TPU v7x, 32 devices: a whole 2x2x4 slice. The times are simulated.
32 devices in a mesh: groups: 2 (over x), shard: 16 (over z, y, core).
Axes of the slice: x: 2, y: 2, z: 4, core: 2. Of those that a mesh axis runs over, the one named last changes fastest.
Arguments:
- features: bfloat16 [8192, 4096], P(('groups', 'shard')), parts along dimension 0, may hold values from -6 to 6
- cotangent: bfloat16 [8192, 4096], P(('groups', 'shard')), parts along dimension 0, may hold values from -0.029907227 to 0.029907227
- member_weight: bfloat16 [1024, 4096], P('shard'), may hold values from -0.1875 to 0.1875
- shared_weight: bfloat16 [256, 2048], P('shard'), may hold values from -0.375 to 0.375
- shared_coords: int32 [8, 2], replicated, may hold values from 0 to 15, as said below
Outputs:
- activated: bfloat16 [8192, 4096], P(('groups', 'shard')), parts along dimension 0
- member_grad: float32 [2048, 4096], P(('groups', 'shard')), parts along dimension 0
- shared_grad: float32 [512, 2048], P(('groups', 'shard')), parts along dimension 0
There are 2 independent parts, one for each index of `groups`. A program takes and returns all parts, laid end to end along the dimension named above; an argument that names none is the same for every part. Nothing has to cross between parts.
Inputs may be any that keep to these rules, and one draw needn't show every extreme that they name: `shared_coords`: the 8 pairs (row block, column block) are distinct, and none lies in a member's diagonal square: row block // 4 differs from column block // 4.
All inputs are finite; a program needn't handle non-finite values.
Results may differ from a plain program's by a relative error of at most 0.0029.
Values may be sent and summed in bfloat16 or wider, within the bound.
A program may use at most 128 MiB of HBM per device.

v0:
```python
import jax
import jax.numpy as jnp
from jax import lax
from jax.sharding import PartitionSpec as P

ROOT_HALF = 0.7071067811865476
INV_ROOT_TWO_PI = 0.3989422804014327


def gelu_slope(hidden):
    return 0.5 * (
        1.0 + jax.scipy.special.erf(hidden * ROOT_HALF)
    ) + hidden * INV_ROOT_TWO_PI * jnp.exp(-0.5 * hidden * hidden)


def member_product(inputs, weights):
    return lax.dot_general(
        inputs, weights, (((2,), (0,)), ((1,), (1,))), preferred_element_type=jnp.float32
    )


def per_device(features, cotangent, member_weight, shared_weight, shared_coords):
    shard_count = lax.axis_size("shard")
    token_rows = features.shape[0]
    width = features.shape[1]
    local_rows = member_weight.shape[0]
    member_width = local_rows * shard_count
    members = width // member_width
    block = shared_weight.shape[0] * shard_count
    shared_count = shared_coords.shape[0]
    grid = width // block
    row_blocks = shared_coords[:, 0]
    col_blocks = shared_coords[:, 1]
    col_onehot = (col_blocks[:, None] == jnp.arange(grid, dtype=jnp.int32)[None, :]).astype(
        jnp.float32
    )
    feat_members = features.reshape(token_rows, members, member_width)
    feat_blocks = jnp.take(features.reshape(token_rows, grid, block), row_blocks, axis=1)
    shared_full = lax.all_gather(shared_weight, "shard", axis=0, tiled=True)
    shared_blocks = shared_full.reshape(block, shared_count, block)
    member_full = lax.all_gather(member_weight, "shard", axis=0, tiled=True)
    member_out = member_product(
        feat_members, member_full.reshape(member_width, members, member_width)
    )
    shared_out = lax.dot_general(
        feat_blocks, shared_blocks, (((2,), (0,)), ((1,), (1,))), preferred_element_type=jnp.float32
    )
    placed = jnp.einsum("stj,sk->tkj", shared_out, col_onehot, precision=lax.Precision.HIGHEST)
    hidden = jnp.transpose(member_out, (1, 0, 2)).reshape(token_rows, width) + placed.reshape(
        token_rows, width
    )
    activated = jax.nn.gelu(hidden, approximate=False).astype(jnp.bfloat16)
    grad_hidden = (cotangent.astype(jnp.float32) * gelu_slope(hidden)).astype(jnp.bfloat16)
    grad_members = grad_hidden.reshape(token_rows, members, member_width)
    grad_blocks = jnp.take(grad_hidden.reshape(token_rows, grid, block), col_blocks, axis=1)
    shared_term = lax.dot_general(
        feat_blocks, grad_blocks, (((0,), (0,)), ((1,), (1,))), preferred_element_type=jnp.float32
    )
    shared_term = jnp.transpose(shared_term, (1, 0, 2)).reshape(block, shared_count * block)
    ratio = member_width // block
    folded = shared_term.reshape(member_width, shared_count * block // ratio)
    term = lax.dot_general(
        feat_members, grad_members, (((0,), (0,)), ((1,), (1,))), preferred_element_type=jnp.float32
    )
    joint = lax.psum_scatter(
        jnp.concatenate(
            [
                jnp.transpose(term, (1, 0, 2)).reshape(lax.axis_size("shard") * local_rows, width),
                folded,
            ],
            axis=1,
        ),
        "shard",
        scatter_dimension=0,
        tiled=True,
    )
    member_grad = joint[:, :width]
    shared_grad = joint[:, width:].reshape(local_rows // ratio, shared_count * block)
    return (activated, member_grad, shared_grad)


def solution(mesh):
    return jax.shard_map(
        per_device,
        mesh=mesh,
        in_specs=(
            P(("groups", "shard"), None),
            P(("groups", "shard"), None),
            P("shard", None),
            P("shard", None),
            P(),
        ),
        out_specs=(
            P(("groups", "shard"), None),
            P(("groups", "shard"), None),
            P(("groups", "shard"), None),
        ),
        check_vma=False,
    )
```

profile of v0, /device:TPU:0, one launch (start us, length us, event | category | flops | bytes accessed | tf_op | source)
XLA Modules:
  0.0 424.5 jit_solution(14927127992019022304)
XLA Ops:
  7.2 0.0 copy-start
  7.2 0.0 all-gather.5.cloned.1.call-start
  7.2 0.7 all-gather.5.cloned.1.call-update
  7.9 0.0 all-gather.3.cloned.1.call-start
  8.0 0.7 all-gather.3.cloned.1.call-update
  8.7 0.0 reduce-scatter.2.cloned.1.call-start
  8.7 4.1 copy.65
  12.8 0.0 copy-done
  12.8 0.0 copy-start.3
  12.8 2.5 copy.59
  15.3 3.9 copy.60
  19.2 0.0 copy-done.3
  19.2 2.2 gather_fusion
  21.5 29.3 %all-gather.5.cloned.1.call-done = bf16[256,2048]{1,0:T(8,128)(2,1)} async-done(((bf16[16,2048]{1,0:T(8,128)(2,1)}), bf16[256,2048]{1,0:T(8,128)(2,1)}) %all-gather.5.cloned.1.call-update) | async-done | bytes 1048592 | tf_op jit(solution)/shard_map/all_gather | solution.py:39
  50.8 2.3 copy.61
  53.1 1.7 fusion.23
  54.8 4.0 convolution_bitcast_fusion
  58.8 5.4 %copy.75 = f32[256,16,256]{0,2,1:T(8,128)} copy(f32[256,16,256]{2,1,0:T(8,128)} %convolution_bitcast_fusion) | data formatting | bytes 8388608 | tf_op jit(solution)/shard_map/reshape | solution.py:49
  64.2 62.6 %all-gather.3.cloned.1.call-done = bf16[1024,4096]{1,0:T(8,128)(2,1)} async-done(((bf16[64,4096]{1,0:T(8,128)(2,1)}), bf16[1024,4096]{1,0:T(8,128)(2,1)}) %all-gather.3.cloned.1.call-update) | async-done | bytes 8388624 | tf_op jit(solution)/shard_map/all_gather | solution.py:41
  126.9 11.9 %copy.55 = bf16[1024,4096]{0,1:T(8,128)(2,1)} copy(bf16[1024,4096]{1,0:T(8,128)(2,1)} %all-gather.3.cloned.1.call-done) | data formatting | bytes 16777216 | tf_op jit(solution)/shard_map/all_gather | solution.py:41
  138.8 7.7 %convolution_bitcast_fusion.1 = f32[256,4,1024]{2,0,1:T(8,128)} fusion(bf16[1024,4,1024]{0,2,1:T(8,128)(2,1)} %bitcast.55, bf16[32,4,8,1024]{3,2,1,0:T(8,128)(2,1)S(1)} %bitcast.56), kind=kOutput, calls=%fused_computation.30 | convolution fusion | flops 2147483648 | bytes 14680064 | tf_op jit(solution)/shard_map/dot_general | solution.py:17
  146.5 5.4 %copy.58 = f32[256,4,1024]{0,2,1:T(8,128)} copy(f32[256,4,1024]{2,0,1:T(8,128)} %convolution_bitcast_fusion.1) | data formatting | bytes 8388608 | tf_op jit(solution)/shard_map/transpose | solution.py:49
  151.9 13.5 %fusion.7 = (bf16[256,4096]{0,1:T(8,128)(2,1)}, bf16[256,4096]{0,1:T(8,128)(2,1)}) fusion(bf16[256,4096]{0,1:T(8,128)(2,1)} %copy.65, f32[256,16,256]{0,2,1:T(8,128)} %copy.75, f32[256,4,1024]{0,2,1:T(8,128)} %copy.58), kind=kLoop, calls=%fused_computation.12 | loop fusion | flops 80740352 | bytes 14680064 | tf_op jit(solution)/shard_map/convert_element_type | solution.py:53
  165.4 3.9 copy.67
  169.3 3.2 gather_fusion.1
  172.5 1.8 convolution_bitcast_fusion.2
  174.3 2.5 copy.69
  176.8 2.9 reshape_reshape.3
  179.7 9.7 %fusion.15 = f32[4,1024,1024]{2,1,0:T(8,128)} fusion(bf16[256,4,1024]{0,2,1:T(8,128)(2,1)} %bitcast.59, bf16[32,4,8,1024]{3,2,1,0:T(8,128)(2,1)S(1)} %bitcast.57), kind=kOutput, calls=%fused_computation.31 | convolution fusion | flops 2147483648 | bytes 20971520 | tf_op jit(solution)/shard_map/dot_general | solution.py:62
  189.4 0.0 copy-start.2
  189.4 17.6 %copy.70 = f32[1024,4096]{1,0:T(8,128)} copy(f32[1024,4096]{0,1:T(8,128)} %bitcast.54) | data formatting | bytes 33554432 | tf_op jit(solution)/shard_map/reshape | solution.py:68
  207.0 0.0 copy-done.2
  207.0 13.7 %pad_maximum_fusion = f32[1024,4608]{1,0:T(8,128)} fusion(f32[1024,512]{1,0:T(8,128)S(1)} %copy-done.2, f32[1024,4096]{1,0:T(8,128)} %copy.70), kind=kLoop, calls=%fused_computation.2 | loop fusion | flops 4718592 | bytes 37748736 | tf_op jit(solution)/shard_map/concatenate | solution.py:66
  220.7 0.0 copy-start.1
  220.7 0.0 reduce-scatter.2.cloned.1.call-update
  220.8 1.6 copy-done.1
  222.3 2.8 copy.71
  225.2 188.9 %reduce-scatter.2.cloned.1.call-done = f32[64,4608]{1,0:T(8,128)} async-done(((f32[1024,4608]{1,0:T(8,128)}), f32[64,4608]{1,0:T(8,128)}) %reduce-scatter.2.cloned.1.call-update) | async-done | bytes 1179664 | tf_op jit(solution)/shard_map/reduce_scatter | solution.py:65
  414.1 0.9 slice.21
  415.0 0.7 reshape.50
  415.7 2.3 slice.20
  (4 shorter events, 0.0 us)
Async XLA Ops:
  7.2 5.6 %copy-start = (bf16[256,4096]{1,0:T(8,128)(2,1)S(1)}, bf16[256,4096]{1,0:T(8,128)(2,1)}, u32[]{:S(2)}) copy-start(bf16[256,4096]{1,0:T(8,128)(2,1)} %param.7) | copy-start | bytes 6291460
  7.2 43.7 %all-gather.5.cloned.1.call-start = ((), (), s32[]{:S(2)}) async-start(), calls=%async_computation.2 | async-start | bytes 1114112 | tf_op jit(solution)/shard_map/all_gather | solution.py:39
  7.9 118.9 %all-gather.3.cloned.1.call-start = ((), (), s32[]{:S(2)}) async-start(), calls=%async_computation.1 | async-start | bytes 8912896 | tf_op jit(solution)/shard_map/all_gather | solution.py:41
  8.7 405.5 %reduce-scatter.2.cloned.1.call-start = ((), (), s32[]{:S(2)}) async-start(), calls=%async_computation.3 | async-start | bytes 20054016 | tf_op jit(solution)/shard_map/reduce_scatter | solution.py:65
  12.8 6.4 %copy-start.3 = (s32[8,2]{0,1:T(2,128)S(1)}, s32[8,2]{0,1:T(2,128)}, u32[]{:S(2)}) copy-start(s32[8,2]{0,1:T(2,128)} %param.11) | copy-start | bytes 196
  189.4 17.6 %copy-start.2 = (f32[1024,512]{1,0:T(8,128)S(1)}, f32[1024,512]{1,0:T(8,128)}, u32[]{:S(2)}) copy-start(f32[1024,512]{1,0:T(8,128)} %reshape_reshape.3) | copy-start | bytes 6291460
  220.7 1.6 copy-start.1
Sparse Core Ops, SparseCore 0:
  10.2 40.6 all-gather.4
  53.0 73.8 all-gather.2
  220.9 193.1 reduce-scatter.1
where the time goes:
time: 426 us; the launch traced here: 425 us
  waiting for transfers between devices  282 us (66%)
  local copies, waits for them, and re-layouts  76.1 us (18%)
  other arithmetic  27.2 us (6%)
  matrix products  24.9 us (6%)
  between operations  13.8 us (3%)
    reduce_scatter x1, waiting for transfers between devices, per_device(): lax.psum_scatter(jnp.concatenate([jnp.transpose(term, (1, 0, 2)).reshape(...  189 us
    all_gather x1, waiting for transfers between devices, per_device(): member_full = lax.all_gather(member_weight, 'shard', axis=0, tiled=True)  62.6 us
    all_gather x1, waiting for transfers between devices, per_device(): shared_full = lax.all_gather(shared_weight, 'shard', axis=0, tiled=True)  29.3 us
    reshape x1, local copies, waits for them, and re-layouts, per_device(): jnp.transpose(term, (1, 0, 2))  17.6 us
    concatenate x1, other arithmetic, per_device(): jnp.concatenate([jnp.transpose(term, (1, 0, 2)).reshape(lax.axis_size('sh...  13.7 us
    convert_element_type x1, other arithmetic, per_device(): (cotangent.astype(jnp.float32) * gelu_slope(hidden)).astype(jnp.bfloat16)  13.5 us
    all_gather x1, local copies, waits for them, and re-layouts, per_device(): member_full = lax.all_gather(member_weight, 'shard', axis=0, tiled=True)  11.9 us
    unnamed x11, local copies, waits for them, and re-layouts  11 us
  transfers between devices with their start and end apart: 3, of which 3 were waited for; matrix products, arithmetic and copies ran while one was open for 7% of the time, Pallas kernels for 0%

commit v1 on v0

v1 whole, which is shorter than its diff:
```python
import functools

import jax
import jax.numpy as jnp
from jax import lax
from jax.experimental import pallas as pl
from jax.experimental.pallas import tpu as pltpu
from jax.sharding import PartitionSpec as P

ROOT_HALF = 0.7071067811865476
INV_ROOT_TWO_PI = 0.3989422804014327
MESH = pl.DeviceIdType.MESH
VMEM_BYTES = 56 * 2**20


def reversed_bits(value, bits):
    out = 0
    for b in range(bits):
        out = out + ((value // 2**b) % 2) * 2 ** (bits - 1 - b)
    return out


def flipped(value, b):
    return value + (1 - 2 * ((value // 2**b) % 2)) * 2**b


def greet(me, bits):
    barrier = pltpu.get_barrier_semaphore()
    for b in range(bits):
        pl.semaphore_signal(
            barrier, inc=1, device_id={"shard": flipped(me, b)}, device_id_type=MESH
        )
    pl.semaphore_wait(barrier, bits)


def gather_kernel(bits, chunks, chunk, member_ref, folded_ref, out_ref, send, recv, local):
    me = lax.axis_index("shard")
    pos = reversed_bits(me, bits)
    greet(me, bits)

    def own(c):
        if c == chunks - 1:
            return folded_ref
        return member_ref.at[:, c * chunk : (c + 1) * chunk]

    def copy(c, k):
        if k == 0:
            src, dst = own(c), out_ref.at[c, pos]
        else:
            src = dst = out_ref.at[c, pl.ds((pos // 2**k) * 2**k, 2**k)]
        return pltpu.make_async_remote_copy(
            src_ref=src,
            dst_ref=dst,
            send_sem=send.at[c, k],
            recv_sem=recv.at[c, k],
            device_id={"shard": flipped(me, bits - 1 - k)},
            device_id_type=MESH,
        )

    def local_copy(c):
        return pltpu.make_async_copy(own(c), out_ref.at[c, pos], local.at[c])

    for wave in range(chunks + bits):
        for k in range(bits + 1):
            c = wave - k
            if c < 0 or c >= chunks:
                continue
            if k == 0:
                local_copy(c).start()
            if k == 1:
                local_copy(c).wait()
            if k > 0:
                copy(c, k - 1).wait_recv()
            if k < bits:
                copy(c, k).start()
    for c in range(chunks):
        for k in range(bits):
            copy(c, k).wait_send()


def layer_kernel(
    bits, block, coords_ref, feat_ref, feat_m_ref, cot_ref, w_ref, s_ref,
    act_ref, term_ref, sterm_ref, hid_ref,
):
    step = pl.program_id(0)
    count = 2**bits
    rows = w_ref.shape[2]
    chunk = w_ref.shape[3]
    shared_count = s_ref.shape[0]
    per = chunk // block
    weights = jnp.concatenate(
        [w_ref[0, reversed_bits(d, bits)] for d in range(count)], axis=0
    )
    hid_ref[...] = jnp.dot(feat_m_ref[...], weights, preferred_element_type=jnp.float32)

    def shared_inputs(s):
        start = pl.multiple_of(coords_ref[s, 0] * block, block)
        return feat_ref[:, pl.ds(start, block)]

    for s in range(shared_count):
        for part in range(per):
            @pl.when(coords_ref[s, 1] == step * per + part)
            def _():
                cols = slice(part * block, (part + 1) * block)
                hid_ref[:, cols] += jnp.dot(
                    shared_inputs(s), s_ref[s], preferred_element_type=jnp.float32
                )

    hidden = hid_ref[...]
    phi = 0.5 * (1.0 + lax.erf(hidden * ROOT_HALF))
    act_ref[...] = (hidden * phi).astype(act_ref.dtype)
    slope = phi + hidden * INV_ROOT_TWO_PI * jnp.exp(-0.5 * hidden * hidden)
    grad = (cot_ref[...].astype(jnp.float32) * slope).astype(jnp.bfloat16)
    term = lax.dot_general(
        feat_m_ref[...], grad, (((0,), (0,)), ((), ())), preferred_element_type=jnp.float32
    )
    for d in range(count):
        term_ref[0, reversed_bits(d, bits)] = term[d * rows : (d + 1) * rows]
    for s in range(shared_count):
        for part in range(per):
            @pl.when(coords_ref[s, 1] == step * per + part)
            def _():
                sterm_ref[s] = lax.dot_general(
                    shared_inputs(s),
                    grad[:, part * block : (part + 1) * block],
                    (((0,), (0,)), ((), ())),
                    preferred_element_type=jnp.float32,
                )


def scatter_kernel(
    bits, chunks, chunk, term_ref, folded_ref, member_out, folded_out, acc, out_buf, in_buf,
    send, recv, local,
):
    me = lax.axis_index("shard")
    pos = reversed_bits(me, bits)
    count = 2**bits

    def load(c):
        src = folded_ref if c == chunks - 1 else term_ref.at[c]
        return pltpu.make_async_copy(src, acc.at[c], local.at[c])

    for c in range(chunks):
        load(c).start()
    greet(me, bits)

    def span(k):
        size = count // 2 ** (k + 1)
        return count - count // 2**k, size

    def copy(c, k):
        first, size = span(k)
        return pltpu.make_async_remote_copy(
            src_ref=out_buf.at[c, pl.ds(first, size)],
            dst_ref=in_buf.at[c, pl.ds(first, size)],
            send_sem=send.at[c, k],
            recv_sem=recv.at[c, k],
            device_id={"shard": flipped(me, k)},
            device_id_type=MESH,
        )

    for wave in range(chunks + bits):
        for k in range(bits + 1):
            c = wave - k
            if c < 0 or c >= chunks:
                continue
            if k == 0:
                load(c).wait()
            else:
                copy(c, k - 1).wait_recv()
                first, size = span(k - 1)
                kept = (pos // size) * size

                @pl.loop(0, size)
                def _(i):
                    acc[c, kept + i] += in_buf[c, first + i].astype(jnp.float32)

            if k < bits:
                first, size = span(k)
                leaving = (flipped(pos, bits - 1 - k) // size) * size

                @pl.loop(0, size)
                def _(i):
                    out_buf[c, first + i] = acc[c, leaving + i].astype(out_buf.dtype)

                copy(c, k).start()
            elif c == chunks - 1:
                folded_out[...] = acc[c, pos]
            else:
                member_out[:, c * chunk : (c + 1) * chunk] = acc[c, pos]
    for c in range(chunks):
        for k in range(bits):
            copy(c, k).wait_send()


def per_device(features, cotangent, member_weight, shared_weight, shared_coords):
    count = lax.axis_size("shard")
    bits = count.bit_length() - 1
    tokens, width = features.shape
    rows = member_weight.shape[0]
    member_width = rows * count
    local = shared_weight.shape[0]
    block = local * count
    shared_count = shared_coords.shape[0]
    ratio = member_width // block
    chunk = shared_count * block // ratio
    member_chunks = width // chunk
    chunks = member_chunks + 1
    per = chunk // block
    f32 = jnp.float32
    any_space = pl.BlockSpec(memory_space=pl.ANY)
    vmem_space = pl.BlockSpec(memory_space=pltpu.VMEM)

    folded = jnp.transpose(shared_weight.reshape(local, ratio, chunk), (1, 0, 2)).reshape(rows, chunk)
    gathered = pl.pallas_call(
        functools.partial(gather_kernel, bits, chunks, chunk),
        out_shape=jax.ShapeDtypeStruct((chunks, count, rows, chunk), jnp.bfloat16),
        in_specs=[any_space, any_space],
        out_specs=any_space,
        scratch_shapes=[
            pltpu.SemaphoreType.DMA((chunks, bits)),
            pltpu.SemaphoreType.DMA((chunks, bits)),
            pltpu.SemaphoreType.DMA((chunks,)),
        ],
        compiler_params=pltpu.CompilerParams(collective_id=0, has_side_effects=True),
        name="gather_weights",
    )(member_weight, folded)

    order = [reversed_bits(d, bits) for d in range(count)]
    twos = (2,) * bits
    back = tuple(reversed(range(bits)))
    shared_pieces = gathered[member_chunks].reshape(twos + (ratio, local, per, block))
    shared_blocks = jnp.transpose(
        shared_pieces, (bits, bits + 2) + back + (bits + 1, bits + 3)
    ).reshape(shared_count, block, block)

    member_chunk_count = member_width // chunk
    activated, term, shared_term = pl.pallas_call(
        functools.partial(layer_kernel, bits, block),
        grid_spec=pltpu.PrefetchScalarGridSpec(
            num_scalar_prefetch=1,
            grid=(member_chunks,),
            in_specs=[
                pl.BlockSpec((tokens, width), lambda j, coords: (0, 0)),
                pl.BlockSpec((tokens, member_width), lambda j, coords: (0, j // member_chunk_count)),
                pl.BlockSpec((tokens, chunk), lambda j, coords: (0, j)),
                pl.BlockSpec((1, count, rows, chunk), lambda j, coords: (j, 0, 0, 0)),
                pl.BlockSpec((shared_count, block, block), lambda j, coords: (0, 0, 0)),
            ],
            out_specs=[
                pl.BlockSpec((tokens, chunk), lambda j, coords: (0, j)),
                pl.BlockSpec((1, count, rows, chunk), lambda j, coords: (j, 0, 0, 0)),
                pl.BlockSpec((shared_count, block, block), lambda j, coords: (0, 0, 0)),
            ],
            scratch_shapes=[pltpu.VMEM((tokens, chunk), f32)],
        ),
        out_shape=[
            jax.ShapeDtypeStruct((tokens, width), jnp.bfloat16),
            jax.ShapeDtypeStruct((member_chunks, count, rows, chunk), f32),
            jax.ShapeDtypeStruct((shared_count, block, block), f32),
        ],
        compiler_params=pltpu.CompilerParams(
            dimension_semantics=("arbitrary",), vmem_limit_bytes=VMEM_BYTES
        ),
        name="layer",
    )(shared_coords, features, features, cotangent, gathered, shared_blocks)

    shared_rows = shared_term.reshape((ratio, per) + twos + (local, block))
    folded_term = jnp.transpose(
        shared_rows, tuple(2 + b for b in back) + (0, bits + 2, 1, bits + 3)
    ).reshape(count, rows, chunk)

    member_grad, folded_grad = pl.pallas_call(
        functools.partial(scatter_kernel, bits, chunks, chunk),
        out_shape=[
            jax.ShapeDtypeStruct((rows, width), f32),
            jax.ShapeDtypeStruct((rows, chunk), f32),
        ],
        in_specs=[any_space, any_space],
        out_specs=[vmem_space, vmem_space],
        scratch_shapes=[
            pltpu.VMEM((chunks, count, rows, chunk), f32),
            pltpu.VMEM((chunks, count, rows, chunk), jnp.bfloat16),
            pltpu.VMEM((chunks, count, rows, chunk), jnp.bfloat16),
            pltpu.SemaphoreType.DMA((chunks, bits)),
            pltpu.SemaphoreType.DMA((chunks, bits)),
            pltpu.SemaphoreType.DMA((chunks,)),
        ],
        compiler_params=pltpu.CompilerParams(
            collective_id=1, has_side_effects=True, vmem_limit_bytes=VMEM_BYTES
        ),
        name="scatter_gradients",
    )(term, folded_term)
    shared_grad = jnp.transpose(folded_grad.reshape(ratio, local, chunk), (1, 0, 2)).reshape(
        local, shared_count * block
    )
    return (activated, member_grad, shared_grad)


def solution(mesh):
    return jax.shard_map(
        per_device,
        mesh=mesh,
        in_specs=(
            P(("groups", "shard"), None),
            P(("groups", "shard"), None),
            P("shard", None),
            P("shard", None),
            P(),
        ),
        out_specs=(
            P(("groups", "shard"), None),
            P(("groups", "shard"), None),
            P(("groups", "shard"), None),
        ),
        check_vma=False,
    )
```

time: 426 us -> 176 us (0.41)
  waiting for transfers between devices: 282 us -> 0 us
  Pallas kernels: 0 us -> 160 us
  local copies, waits for them, and re-layouts: 76.1 us -> 15.6 us
  other arithmetic: 27.2 us -> 0 us
  matrix products: 24.9 us -> 0 us
  between operations: 13.8 us -> 0.67 us
    reduce_scatter x1 -> x0, waiting for transfers between devices: 189 us -> none  [per_device(): lax.psum_scatter(jnp.concatenate([jnp.transpose(term, (1, 0, 2)).reshape(...]
    pallas_call x0 -> x3, Pallas kernels: none -> 160 us  [the longest x1 71.6 us: per_device(): pl.pallas_call(functools.partial(gather_kernel, bits, chunks, chunk), out...]
    all_gather x2 -> x0, waiting for transfers between devices: 92 us -> none  [the longest x1 62.6 us: per_device(): member_full = lax.all_gather(member_weight, 'shard', axis=0, tiled=True)]
    dot_general x5 -> x0, matrix products: 24.9 us -> none  [the longest x1 9.68 us: per_device(): lax.dot_general(feat_members, grad_members, (((0,), (0,)), ((1,), (1,))),...]
    reshape x5 -> x4, local copies, waits for them, and re-layouts: 31.5 us -> 9.27 us  [the longest x1 3.5 us: per_device(): shared_rows = shared_term.reshape((ratio, per) + twos + (local, block))]
    all_gather x2 -> x0, local copies, waits for them, and re-layouts: 14.2 us -> none  [the longest x1 11.9 us: per_device(): member_full = lax.all_gather(member_weight, 'shard', axis=0, tiled=True)]
    concatenate x1 -> x0, other arithmetic: 13.7 us -> none  [per_device(): jnp.concatenate([jnp.transpose(term, (1, 0, 2)).reshape(lax.axis_size('sh...]
    convert_element_type x1 -> x0, other arithmetic: 13.5 us -> none  [per_device(): (cotangent.astype(jnp.float32) * gelu_slope(hidden)).astype(jnp.bfloat16)]
  transfers between devices with their start and end apart: 3 -> 0, of which waited for: 3 -> 0; matrix products, arithmetic and copies ran while one was open for 7% -> 0% of each run, Pallas kernels for 0% -> 0%
where the time goes in v1:
time: 176 us
  Pallas kernels  160 us (91%)
  local copies, waits for them, and re-layouts  15.6 us (9%)
    pallas_call x1, Pallas kernels, per_device(): pl.pallas_call(functools.partial(gather_kernel, bits, chunks, chunk), out...  71.6 us
    pallas_call x1, Pallas kernels, per_device(): pl.pallas_call(functools.partial(scatter_kernel, bits, chunks, chunk), ou...  66.4 us
    pallas_call x1, Pallas kernels, per_device(): pl.pallas_call(functools.partial(layer_kernel, bits, block), grid_spec=pl...  21.7 us
    unnamed x2, local copies, waits for them, and re-layouts  3.61 us

profile of v1, /device:TPU:0, one launch (start us, length us, event | category | flops | bytes accessed | tf_op | source)
XLA Modules:
  0.0 175.9 jit_solution(14606906273227399867)
XLA Ops:
  0.6 1.3 copy.10.coords_ref
  2.0 1.5 copy.18
  3.4 71.6 %gather_weights.1.w_ref = bf16[9,16,64,512]{3,2,1,0:T(8,128)(2,1)} custom-call(bf16[64,4096]{1,0:T(8,128)(2,1)} %member_ref.1, bf16[64,512]{1,0:T(8,128)(2,1)} %bitcast.24), custom_call_target="tpu_custom_call" | custom-call | tf_op jit(solution)/shard_map/gather_weights/pallas_call | solution.py:215
  75.0 0.0 slice-start
  75.0 1.2 slice-done
  76.3 0.3 reshape_squeeze.3
  76.5 1.2 copy.9
  77.7 21.7 %layer.1 = (bf16[256,4096]{1,0:T(8,128)(2,1)}, f32[8,16,64,512]{3,2,1,0:T(8,128)}, f32[8,256,256]{2,1,0:T(8,128)}) custom-call(s32[8,2]{1,0:T(8,128)} %copy.10.coords_ref, bf16[256,4096]{1,0:T(8,128)(2,1)} %feat_m_ref.1, bf16[256,4096]{1,0:T(8,128)(2,1)} %feat_m_ref.1, bf16[256,4096]{1,0:T(8,128)(2,1)} %cot_ref.1, ...), custom_call_target="tpu_custom_call" | custom-call | tf_op jit(solution)/shard_map/layer/pallas_call | solution.py:238
  99.4 3.5 %copy.17 = f32[4,2,2,2,2,2,16,256]{7,1,6,0,2,3,4,5:T(2,128)S(1)} copy(f32[4,2,2,2,2,2,16,256]{7,6,5,4,3,2,1,0:T(8,128)} %bitcast.23) | data formatting | bytes 4194304 | tf_op jit(solution)/shard_map/reshape | solution.py:268
  103.0 2.7 %reshape.31.folded_ref = f32[16,64,512]{2,1,0:T(8,128)} reshape(f32[2,2,2,2,4,16,2,256]{7,6,5,4,3,2,1,0:T(2,128)S(1)} %bitcast.21) | data formatting | bytes 4194304 | tf_op jit(solution)/shard_map/reshape | solution.py:271
  105.7 66.4 %scatter_gradients.1 = (f32[64,4096]{1,0:T(8,128)}, f32[64,512]{1,0:T(8,128)}) custom-call(f32[8,16,64,512]{3,2,1,0:T(8,128)} %get-tuple-element.9.term_ref, f32[16,64,512]{2,1,0:T(8,128)} %reshape.31.folded_ref), custom_call_target="tpu_custom_call" | custom-call | tf_op jit(solution)/shard_map/scatter_gradients/pallas_call | solution.py:273
  172.1 1.6 copy.14
  173.7 2.3 %copy.20 = f32[64,4096]{1,0:T(8,128)} copy(f32[64,4096]{1,0:T(8,128)} %get-tuple-element.17) | data formatting | bytes 2097152
Async XLA Ops:
  75.0 1.2 slice-start

commit v2 on v0

v2 whole, which is shorter than its diff:
```python
import functools

import jax
import jax.numpy as jnp
from jax import lax
from jax.experimental import pallas as pl
from jax.experimental.pallas import tpu as pltpu
from jax.sharding import PartitionSpec as P

ROOT_HALF = 0.7071067811865476
INV_ROOT_TWO_PI = 0.3989422804014327
MESH = pl.DeviceIdType.MESH
VMEM_BYTES = 60 * 2**20


def reversed_bits(value, bits):
    out = 0
    for b in range(bits):
        out = out + ((value // 2**b) % 2) * 2 ** (bits - 1 - b)
    return out


def flipped(value, b):
    return value + (1 - 2 * ((value // 2**b) % 2)) * 2**b


def fused_kernel(
    bits, twin, block, shared_count, table_ref, feat_hbm, cot_hbm, member_ref, folded_ref,
    act_hbm, member_out, folded_out,
    feat, cot, grad, act, gathered, acc, out_buf, in_buf, sums,
    own_sem, load_sem, act_sem, gather_send, gather_recv, send, recv,
):
    me = lax.axis_index("shard")
    group = lax.axis_index("groups")
    pos = reversed_bits(me, bits)
    count = 2**bits
    items, _, rows, chunk = gathered.shape
    member_chunks = items - 1
    slots = acc.shape[0]
    per = chunk // block
    ratio = shared_count // per
    local = rows // ratio
    member_width = rows * count
    grid, tokens = feat.shape[:2]
    f32 = jnp.float32
    at_col, at_before, at_last = shared_count, 2 * shared_count, 3 * shared_count

    def peer(b):
        return {"shard": flipped(me, b)}

    across = {"groups": flipped(group, 0)}
    half = group % 2
    stages = []
    for k in range(bits):
        b = bits - 1 - k
        start, size = (pos // 2**k) * 2**k, 2**k
        if b == 1 and twin:
            size //= 2
            stages.append((start + half * size, size, peer(b)))
            there = (flipped(pos, k) // 2**k) * 2**k
            stages.append((there + half * size, size, across))
        else:
            stages.append((start, size, peer(b)))
    ahead = len(stages)

    def gather_copy(g, k):
        start, size, target = stages[k]
        part = gathered.at[g, pl.ds(start, size)]
        return pltpu.make_async_remote_copy(
            src_ref=part,
            dst_ref=part,
            send_sem=gather_send.at[g, k],
            recv_sem=gather_recv.at[g, k],
            device_id=target,
            device_id_type=MESH,
        )

    def span(k):
        size = count // 2 ** (k + 1)
        return count - count // 2**k, size

    def scatter_copy(h, k):
        first, size = span(k)
        return pltpu.make_async_remote_copy(
            src_ref=out_buf.at[h, pl.ds(first, size)],
            dst_ref=in_buf.at[h, pl.ds(first, size)],
            send_sem=send.at[h, k],
            recv_sem=recv.at[h, k],
            device_id=peer(k),
            device_id_type=MESH,
        )

    def columns(j):
        return pl.ds(pl.multiple_of(j * chunk, chunk), chunk)

    def act_copy(j):
        return pltpu.make_async_copy(act.at[j], act_hbm.at[:, columns(j)], act_sem.at[j])

    own = [pltpu.make_async_copy(folded_ref, gathered.at[0, pos], own_sem.at[0])]
    for j in range(member_chunks):
        own.append(
            pltpu.make_async_copy(
                member_ref.at[:, j * chunk : (j + 1) * chunk],
                gathered.at[j + 1, pos],
                own_sem.at[j + 1],
            )
        )
    loads = [pltpu.make_async_copy(cot_hbm, cot, load_sem.at[grid])]
    for i in range(grid):
        loads.append(
            pltpu.make_async_copy(
                feat_hbm.at[:, i * block : (i + 1) * block], feat.at[i], load_sem.at[i]
            )
        )
    for copy in own + loads:
        copy.start()

    barrier = pltpu.get_barrier_semaphore()
    partners = [peer(b) for b in range(bits)] + ([across] if twin else [])
    for target in partners:
        pl.semaphore_signal(barrier, inc=1, device_id=target, device_id_type=MESH)
    pl.semaphore_wait(barrier, len(partners))
    for copy in own:
        copy.wait()

    def shared_inputs(s):
        return feat[table_ref[s]]

    def place(s):
        return s // per, slice((s % per) * block, (s % per + 1) * block)

    def shared_forward():
        @pl.loop(0, count)
        def _(i):
            acc[0, i] = gathered[0, i].astype(f32)

        for q in range(ratio):
            for d in range(count):
                row = q * block + d * local
                acc[1, row // rows, row % rows : row % rows + local] = acc[
                    0, reversed_bits(d, bits), q * local : (q + 1) * local
                ]
        sums[shared_count] = jnp.zeros((tokens, block), f32)
        pieces = block // rows
        for s in range(shared_count):
            q, cols = place(s)
            weights = jnp.concatenate(
                [acc[1, q * pieces + i, :, cols] for i in range(pieces)], axis=0
            ).astype(jnp.bfloat16)
            sums[s] = sums[table_ref[at_before + s]] + jnp.dot(
                shared_inputs(s), weights, preferred_element_type=f32
            )

    def member_step(j):
        across_member = member_width // block
        member = (j * chunk // member_width) * across_member
        inputs = jnp.concatenate([feat[member + i] for i in range(across_member)], axis=1)
        weights = jnp.concatenate(
            [gathered[j + 1, reversed_bits(d, bits)] for d in range(count)], axis=0
        )
        hidden = jnp.dot(inputs, weights, preferred_element_type=f32)
        hidden = hidden + jnp.concatenate(
            [sums[table_ref[at_last + j * per + part]] for part in range(per)], axis=1
        )
        phi = 0.5 * (1.0 + lax.erf(hidden * ROOT_HALF))
        act[j] = (hidden * phi).astype(act.dtype)
        act_copy(j).start()
        slope = phi + hidden * INV_ROOT_TWO_PI * jnp.exp(-0.5 * hidden * hidden)
        new = (cot[:, columns(j)].astype(f32) * slope).astype(jnp.bfloat16)
        for part in range(per):
            grad[j * per + part] = new[:, part * block : (part + 1) * block]
        term = lax.dot_general(
            inputs, new, (((0,), (0,)), ((), ())), preferred_element_type=f32
        )
        for d in range(count):
            acc[j % slots, reversed_bits(d, bits)] = term[d * rows : (d + 1) * rows]

    def shared_step():
        slot = member_chunks % slots
        for s in range(shared_count):
            q, cols = place(s)
            sums[s] = lax.dot_general(
                shared_inputs(s),
                grad[table_ref[at_col + s]],
                (((0,), (0,)), ((), ())),
                preferred_element_type=f32,
            )
            for d in range(count):
                acc[slot, reversed_bits(d, bits), q * local : (q + 1) * local, cols] = sums[
                    s, d * local : (d + 1) * local
                ]

    def scatter_stage(h, k):
        slot = h % slots
        if k > 0:
            scatter_copy(h, k - 1).wait_recv()
            first, size = span(k - 1)
            kept = (pos // size) * size

            @pl.loop(0, size)
            def _(i):
                acc[slot, kept + i] += in_buf[h, first + i].astype(f32)

        if k < bits:
            first, size = span(k)
            leaving = (flipped(pos, bits - 1 - k) // size) * size

            @pl.loop(0, size)
            def _(i):
                out_buf[h, first + i] = acc[slot, leaving + i].astype(out_buf.dtype)

            scatter_copy(h, k).start()
        else:
            @pl.when(h < member_chunks)
            def _():
                member_out[:, columns(h)] = acc[slot, pos]

            @pl.when(h == member_chunks)
            def _():
                folded_out[...] = acc[slot, pos]

    def when_in_range(index, action):
        @pl.when((index >= 0) & (index < items))
        def _():
            action(index)

    @pl.loop(0, items + ahead + 1 + bits)
    def _(wave):
        for k in range(ahead):
            def gather_stage(g, k=k):
                if k > 0:
                    gather_copy(g, k - 1).wait_recv()
                gather_copy(g, k).start()

            when_in_range(wave - k, gather_stage)
        for k in range(1, bits + 1):
            when_in_range(wave - ahead - 1 - k, functools.partial(scatter_stage, k=k))
        when_in_range(wave - ahead, lambda g: gather_copy(g, ahead - 1).wait_recv())

        @pl.when(wave == ahead)
        def _():
            for copy in loads:
                copy.wait()
            shared_forward()

        @pl.when((wave > ahead) & (wave < ahead + items))
        def _():
            member_step(wave - ahead - 1)

        @pl.when(wave == ahead + items)
        def _():
            shared_step()

        when_in_range(wave - ahead - 1, functools.partial(scatter_stage, k=0))

    @pl.loop(0, items)
    def _(g):
        for k in range(ahead):
            gather_copy(g, k).wait_send()
        for k in range(bits):
            scatter_copy(g, k).wait_send()

    @pl.loop(0, member_chunks)
    def _(j):
        act_copy(j).wait()


def per_device(features, cotangent, member_weight, shared_weight, shared_coords):
    count = lax.axis_size("shard")
    bits = count.bit_length() - 1
    twin = lax.axis_size("groups") % 2 == 0 and bits >= 3
    ahead = bits + int(twin)
    tokens, width = features.shape
    rows = member_weight.shape[0]
    local = shared_weight.shape[0]
    block = local * count
    shared_count = shared_coords.shape[0]
    ratio = rows // local
    chunk = shared_count * block // ratio
    member_chunks = width // chunk
    items = member_chunks + 1
    f32, bf16 = jnp.float32, jnp.bfloat16
    any_space = pl.BlockSpec(memory_space=pl.ANY)
    vmem_space = pl.BlockSpec(memory_space=pltpu.VMEM)

    folded = jnp.transpose(shared_weight.reshape(local, ratio, chunk), (1, 0, 2)).reshape(rows, chunk)
    cols = shared_coords[:, 1]
    order = jnp.arange(shared_count, dtype=jnp.int32)

    def last_with(column, upto):
        hit = (cols[None, :] == column[:, None]) & (order[None, :] < upto[:, None])
        found = jnp.max(jnp.where(hit, order[None, :], -1), axis=1)
        return jnp.where(found < 0, shared_count, found)

    grid = jnp.arange(width // block, dtype=jnp.int32)
    table = jnp.concatenate(
        [
            shared_coords[:, 0],
            cols,
            last_with(
                jnp.concatenate([cols, grid]),
                jnp.concatenate([order, jnp.full_like(grid, shared_count)]),
            ),
        ]
    )
    activated, member_grad, folded_grad = pl.pallas_call(
        functools.partial(fused_kernel, bits, twin, block, shared_count),
        out_shape=[
            jax.ShapeDtypeStruct((tokens, width), bf16),
            jax.ShapeDtypeStruct((rows, width), f32),
            jax.ShapeDtypeStruct((rows, chunk), f32),
        ],
        in_specs=[pl.BlockSpec(memory_space=pltpu.SMEM)] + [any_space] * 4,
        out_specs=[any_space, vmem_space, vmem_space],
        scratch_shapes=[
            pltpu.VMEM((width // block, tokens, block), bf16),
            pltpu.VMEM((tokens, width), bf16),
            pltpu.VMEM((width // block, tokens, block), bf16),
            pltpu.VMEM((member_chunks, tokens, chunk), bf16),
            pltpu.VMEM((items, count, rows, chunk), bf16),
            pltpu.VMEM((bits + 2, count, rows, chunk), f32),
            pltpu.VMEM((items, count, rows, chunk), bf16),
            pltpu.VMEM((items, count, rows, chunk), bf16),
            pltpu.VMEM((shared_count + 1, max(tokens, block), block), f32),
            pltpu.SemaphoreType.DMA((items,)),
            pltpu.SemaphoreType.DMA((width // block + 1,)),
            pltpu.SemaphoreType.DMA((member_chunks,)),
            pltpu.SemaphoreType.DMA((items, ahead)),
            pltpu.SemaphoreType.DMA((items, ahead)),
            pltpu.SemaphoreType.DMA((items, bits)),
            pltpu.SemaphoreType.DMA((items, bits)),
        ],
        compiler_params=pltpu.CompilerParams(
            collective_id=0, has_side_effects=True, vmem_limit_bytes=VMEM_BYTES
        ),
        name="fused_layer",
    )(table, features, cotangent, member_weight, folded)
    shared_grad = jnp.transpose(folded_grad.reshape(ratio, local, chunk), (1, 0, 2)).reshape(
        local, shared_count * block
    )
    return (activated, member_grad, shared_grad)


def solution(mesh):
    return jax.shard_map(
        per_device,
        mesh=mesh,
        in_specs=(
            P(("groups", "shard"), None),
            P(("groups", "shard"), None),
            P("shard", None),
            P("shard", None),
            P(),
        ),
        out_specs=(
            P(("groups", "shard"), None),
            P(("groups", "shard"), None),
            P(("groups", "shard"), None),
        ),
        check_vma=False,
    )
```

time: 426 us -> 124 us (0.29)
  waiting for transfers between devices: 282 us -> 0 us
  Pallas kernels: 0 us -> 114 us
  local copies, waits for them, and re-layouts: 76.1 us -> 7.99 us
  other arithmetic: 27.2 us -> 1.41 us
  matrix products: 24.9 us -> 0 us
  between operations: 13.8 us -> 0.65 us
    reduce_scatter x1 -> x0, waiting for transfers between devices: 189 us -> none  [per_device(): lax.psum_scatter(jnp.concatenate([jnp.transpose(term, (1, 0, 2)).reshape(...]
    pallas_call x0 -> x1, Pallas kernels: none -> 114 us  [per_device(): pl.pallas_call(functools.partial(fused_kernel, bits, twin, block, shared_...]
    all_gather x2 -> x0, waiting for transfers between devices: 92 us -> none  [the longest x1 62.6 us: per_device(): member_full = lax.all_gather(member_weight, 'shard', axis=0, tiled=True)]
    reshape x5 -> x2, local copies, waits for them, and re-layouts: 31.5 us -> 3.04 us  [the longest x1 1.57 us: per_device(): jnp.transpose(folded_grad.reshape(ratio, local, chunk), (1, 0, 2))]
    dot_general x5 -> x0, matrix products: 24.9 us -> none  [the longest x1 9.68 us: per_device(): lax.dot_general(feat_members, grad_members, (((0,), (0,)), ((1,), (1,))),...]
    all_gather x2 -> x0, local copies, waits for them, and re-layouts: 14.2 us -> none  [the longest x1 11.9 us: per_device(): member_full = lax.all_gather(member_weight, 'shard', axis=0, tiled=True)]
    convert_element_type x1 -> x0, other arithmetic: 13.5 us -> none  [per_device(): (cotangent.astype(jnp.float32) * gelu_slope(hidden)).astype(jnp.bfloat16)]
    concatenate x1 -> x2, other arithmetic: 13.7 us -> 0.66 us  [the longest x1 0.59 us: per_device(): jnp.concatenate([shared_coords[:, 0], cols, last_with(jnp.concatenate([co...]
  transfers between devices with their start and end apart: 3 -> 0, of which waited for: 3 -> 0; matrix products, arithmetic and copies ran while one was open for 7% -> 0% of each run, Pallas kernels for 0% -> 0%
where the time goes in v2:
time: 124 us
  Pallas kernels  114 us (92%)
  local copies, waits for them, and re-layouts  7.99 us (6%)
  other arithmetic  1.41 us (1%)
    pallas_call x1, Pallas kernels, per_device(): pl.pallas_call(functools.partial(fused_kernel, bits, twin, block, shared_...  114 us
    unnamed x4, local copies, waits for them, and re-layouts  4.19 us

profile of v2, /device:TPU:0, one launch (start us, length us, event | category | flops | bytes accessed | tf_op | source)
XLA Modules:
  0.0 123.8 jit_solution(7887308778440230551)
XLA Ops:
  0.6 0.8 slice_bitcast_fusion.1
  1.4 0.1 pad_add_fusion
  1.5 0.7 select_reduce_fusion
  2.2 0.6 pad_add_fusion.1.table_ref
  2.8 1.5 %copy.15 = bf16[2,4,8,512]{3,2,0,1:T(8,128)(2,1)} copy(bf16[2,4,8,512]{3,2,1,0:T(8,128)(2,1)} %bitcast.19) | data formatting | bytes 131072 | tf_op jit(solution)/shard_map/reshape | solution.py:286
  4.3 113.7 %fused_layer.1 = (bf16[256,4096]{1,0:T(8,128)(2,1)}, f32[64,4096]{1,0:T(8,128)}, f32[64,512]{1,0:T(8,128)}) custom-call(s32[40]{0:T(128)} %pad_add_fusion.1.table_ref, bf16[256,4096]{1,0:T(8,128)(2,1)} %feat_hbm.1, bf16[256,4096]{1,0:T(8,128)(2,1)} %cot_hbm.1, bf16[64,4096]{1,0:T(8,128)(2,1)} %member_ref.1, bf16[64,512]{1,0:T(8,128)(2,1)} %bitcast.16), custom_call_target="tpu_custom_call" | custom-call | tf_op jit(solution)/shard_map/fused_layer/pallas_call | solution.py:306
  118.0 1.6 %copy.13 = f32[4,2,8,512]{3,2,0,1:T(8,128)} copy(f32[4,2,8,512]{3,2,1,0:T(8,128)} %bitcast.18) | data formatting | bytes 262144 | tf_op jit(solution)/shard_map/reshape | solution.py:338
  119.6 0.0 copy-start
  119.6 3.2 %copy.18 = bf16[256,4096]{1,0:T(8,128)(2,1)} copy(bf16[256,4096]{1,0:T(8,128)(2,1)} %get-tuple-element.14) | data formatting | bytes 4194304
  122.8 0.0 copy-done
  122.8 1.0 copy.19
  (2 shorter events, 0.0 us)
Async XLA Ops:
  119.6 3.2 %copy-start = (f32[64,4096]{1,0:T(8,128)S(1)}, f32[64,4096]{1,0:T(8,128)}, u32[]{:S(2)}) copy-start(f32[64,4096]{1,0:T(8,128)} %get-tuple-element.15) | copy-start | bytes 3145732

commit v3 on v2

--- a/solution.py
+++ b/solution.py
@@ -10,6 +10,7 @@
 ROOT_HALF = 0.7071067811865476
 INV_ROOT_TWO_PI = 0.3989422804014327
 MESH = pl.DeviceIdType.MESH
+CHUNK_BLOCKS = 1
 VMEM_BYTES = 60 * 2**20
 
 
@@ -25,7 +26,7 @@
 
 
 def fused_kernel(
-    bits, twin, block, shared_count, table_ref, feat_hbm, cot_hbm, member_ref, folded_ref,
+    bits, twin, block, shared_items, coords_ref, feat_hbm, cot_hbm, member_ref, folded_ref,
     act_hbm, member_out, folded_out,
     feat, cot, grad, act, gathered, acc, out_buf, in_buf, sums,
     own_sem, load_sem, act_sem, gather_send, gather_recv, send, recv,
@@ -35,15 +36,24 @@
     pos = reversed_bits(me, bits)
     count = 2**bits
     items, _, rows, chunk = gathered.shape
-    member_chunks = items - 1
+    member_chunks = items - shared_items
+    shared_count = coords_ref.shape[0]
     slots = acc.shape[0]
     per = chunk // block
-    ratio = shared_count // per
+    folded_blocks = shared_items * per
+    ratio = shared_count // folded_blocks
     local = rows // ratio
     member_width = rows * count
     grid, tokens = feat.shape[:2]
     f32 = jnp.float32
-    at_col, at_before, at_last = shared_count, 2 * shared_count, 3 * shared_count
+    arrival = [q * folded_blocks + e for e in range(folded_blocks) for q in range(ratio)]
+
+    def last_of(column, positions):
+        found = jnp.int32(0)
+        for t in positions:
+            apart = coords_ref[arrival[t], 1] - column
+            found = jnp.maximum(found, (1 - jnp.minimum(apart * apart, 1)) * (t + 1))
+        return found
 
     def peer(b):
         return {"shard": flipped(me, b)}
@@ -96,13 +106,12 @@
     def act_copy(j):
         return pltpu.make_async_copy(act.at[j], act_hbm.at[:, columns(j)], act_sem.at[j])
 
-    own = [pltpu.make_async_copy(folded_ref, gathered.at[0, pos], own_sem.at[0])]
-    for j in range(member_chunks):
+    own = []
+    for g in range(items):
+        ref, j = (folded_ref, g) if g < shared_items else (member_ref, g - shared_items)
         own.append(
             pltpu.make_async_copy(
-                member_ref.at[:, j * chunk : (j + 1) * chunk],
-                gathered.at[j + 1, pos],
-                own_sem.at[j + 1],
+                ref.at[:, j * chunk : (j + 1) * chunk], gathered.at[g, pos], own_sem.at[g]
             )
         )
     loads = [pltpu.make_async_copy(cot_hbm, cot, load_sem.at[grid])]
@@ -124,30 +133,32 @@
         copy.wait()
 
     def shared_inputs(s):
-        return feat[table_ref[s]]
+        return feat[coords_ref[s, 0]]
 
     def place(s):
-        return s // per, slice((s % per) * block, (s % per + 1) * block)
+        q, e = s // folded_blocks, s % folded_blocks
+        return q, e // per, slice((e % per) * block, (e % per + 1) * block)
 
     def shared_forward():
-        @pl.loop(0, count)
-        def _(i):
-            acc[0, i] = gathered[0, i].astype(f32)
-
-        for q in range(ratio):
-            for d in range(count):
-                row = q * block + d * local
-                acc[1, row // rows, row % rows : row % rows + local] = acc[
-                    0, reversed_bits(d, bits), q * local : (q + 1) * local
-                ]
-        sums[shared_count] = jnp.zeros((tokens, block), f32)
+        sums[0] = jnp.zeros((tokens, block), f32)
         pieces = block // rows
-        for s in range(shared_count):
-            q, cols = place(s)
+        for t, s in enumerate(arrival):
+            q, item, cols = place(s)
+            if t % (ratio * per) == 0:
+                @pl.loop(0, count)
+                def _(i):
+                    acc[0, i] = gathered[item, i].astype(f32)
+
+                for r in range(ratio):
+                    for d in range(count):
+                        row = r * block + d * local
+                        acc[1, row // rows, row % rows : row % rows + local] = acc[
+                            0, reversed_bits(d, bits), r * local : (r + 1) * local
+                        ]
             weights = jnp.concatenate(
                 [acc[1, q * pieces + i, :, cols] for i in range(pieces)], axis=0
             ).astype(jnp.bfloat16)
-            sums[s] = sums[table_ref[at_before + s]] + jnp.dot(
+            sums[t + 1] = sums[last_of(coords_ref[s, 1], range(t))] + jnp.dot(
                 shared_inputs(s), weights, preferred_element_type=f32
             )
 
@@ -156,11 +167,11 @@
         member = (j * chunk // member_width) * across_member
         inputs = jnp.concatenate([feat[member + i] for i in range(across_member)], axis=1)
         weights = jnp.concatenate(
-            [gathered[j + 1, reversed_bits(d, bits)] for d in range(count)], axis=0
+            [gathered[j + shared_items, reversed_bits(d, bits)] for d in range(count)], axis=0
         )
         hidden = jnp.dot(inputs, weights, preferred_element_type=f32)
         hidden = hidden + jnp.concatenate(
-            [sums[table_ref[at_last + j * per + part]] for part in range(per)], axis=1
+            [sums[last_of(j * per + part, range(shared_count))] for part in range(per)], axis=1
         )
         phi = 0.5 * (1.0 + lax.erf(hidden * ROOT_HALF))
         act[j] = (hidden * phi).astype(act.dtype)
@@ -175,13 +186,15 @@
         for d in range(count):
             acc[j % slots, reversed_bits(d, bits)] = term[d * rows : (d + 1) * rows]
 
-    def shared_step():
-        slot = member_chunks % slots
+    def shared_step(item):
+        slot = (member_chunks + item) % slots
         for s in range(shared_count):
-            q, cols = place(s)
+            q, its_item, cols = place(s)
+            if its_item != item:
+                continue
             sums[s] = lax.dot_general(
                 shared_inputs(s),
-                grad[table_ref[at_col + s]],
+                grad[coords_ref[s, 1]],
                 (((0,), (0,)), ((), ())),
                 preferred_element_type=f32,
             )
@@ -215,16 +228,18 @@
             def _():
                 member_out[:, columns(h)] = acc[slot, pos]
 
-            @pl.when(h == member_chunks)
+            @pl.when(h >= member_chunks)
             def _():
-                folded_out[...] = acc[slot, pos]
+                folded_out[:, columns(h - member_chunks)] = acc[slot, pos]
 
     def when_in_range(index, action):
         @pl.when((index >= 0) & (index < items))
         def _():
             action(index)
 
-    @pl.loop(0, items + ahead + 1 + bits)
+    base = ahead + shared_items
+
+    @pl.loop(0, base + items + bits)
     def _(wave):
         for k in range(ahead):
             def gather_stage(g, k=k):
@@ -234,24 +249,25 @@
 
             when_in_range(wave - k, gather_stage)
         for k in range(1, bits + 1):
-            when_in_range(wave - ahead - 1 - k, functools.partial(scatter_stage, k=k))
+            when_in_range(wave - base - k, functools.partial(scatter_stage, k=k))
         when_in_range(wave - ahead, lambda g: gather_copy(g, ahead - 1).wait_recv())
 
-        @pl.when(wave == ahead)
+        @pl.when(wave == base - 1)
         def _():
             for copy in loads:
                 copy.wait()
             shared_forward()
 
-        @pl.when((wave > ahead) & (wave < ahead + items))
+        @pl.when((wave >= base) & (wave < base + member_chunks))
         def _():
-            member_step(wave - ahead - 1)
-
-        @pl.when(wave == ahead + items)
-        def _():
-            shared_step()
-
-        when_in_range(wave - ahead - 1, functools.partial(scatter_stage, k=0))
+            member_step(wave - base)
+
+        for item in range(shared_items):
+            @pl.when(wave == base + member_chunks + item)
+            def _():
+                shared_step(item)
+
+        when_in_range(wave - base, functools.partial(scatter_stage, k=0))
 
     @pl.loop(0, items)
     def _(g):
@@ -276,39 +292,24 @@
     block = local * count
     shared_count = shared_coords.shape[0]
     ratio = rows // local
-    chunk = shared_count * block // ratio
+    folded_width = shared_count * block // ratio
+    chunk = CHUNK_BLOCKS * block
     member_chunks = width // chunk
-    items = member_chunks + 1
+    shared_items = folded_width // chunk
+    items = member_chunks + shared_items
     f32, bf16 = jnp.float32, jnp.bfloat16
     any_space = pl.BlockSpec(memory_space=pl.ANY)
     vmem_space = pl.BlockSpec(memory_space=pltpu.VMEM)
 
-    folded = jnp.transpose(shared_weight.reshape(local, ratio, chunk), (1, 0, 2)).reshape(rows, chunk)
-    cols = shared_coords[:, 1]
-    order = jnp.arange(shared_count, dtype=jnp.int32)
-
-    def last_with(column, upto):
-        hit = (cols[None, :] == column[:, None]) & (order[None, :] < upto[:, None])
-        found = jnp.max(jnp.where(hit, order[None, :], -1), axis=1)
-        return jnp.where(found < 0, shared_count, found)
-
-    grid = jnp.arange(width // block, dtype=jnp.int32)
-    table = jnp.concatenate(
-        [
-            shared_coords[:, 0],
-            cols,
-            last_with(
-                jnp.concatenate([cols, grid]),
-                jnp.concatenate([order, jnp.full_like(grid, shared_count)]),
-            ),
-        ]
+    folded = jnp.transpose(shared_weight.reshape(local, ratio, folded_width), (1, 0, 2)).reshape(
+        rows, folded_width
     )
     activated, member_grad, folded_grad = pl.pallas_call(
-        functools.partial(fused_kernel, bits, twin, block, shared_count),
+        functools.partial(fused_kernel, bits, twin, block, shared_items),
         out_shape=[
             jax.ShapeDtypeStruct((tokens, width), bf16),
             jax.ShapeDtypeStruct((rows, width), f32),
-            jax.ShapeDtypeStruct((rows, chunk), f32),
+            jax.ShapeDtypeStruct((rows, folded_width), f32),
         ],
         in_specs=[pl.BlockSpec(memory_space=pltpu.SMEM)] + [any_space] * 4,
         out_specs=[any_space, vmem_space, vmem_space],
@@ -334,8 +335,8 @@
             collective_id=0, has_side_effects=True, vmem_limit_bytes=VMEM_BYTES
         ),
         name="fused_layer",
-    )(table, features, cotangent, member_weight, folded)
-    shared_grad = jnp.transpose(folded_grad.reshape(ratio, local, chunk), (1, 0, 2)).reshape(
+    )(shared_coords, features, cotangent, member_weight, folded)
+    shared_grad = jnp.transpose(folded_grad.reshape(ratio, local, folded_width), (1, 0, 2)).reshape(
         local, shared_count * block
     )
     return (activated, member_grad, shared_grad)

time: 124 us -> 127 us (1.024)
  Pallas kernels: 114 us -> 118 us
  other arithmetic: 1.41 us -> 0 us
    pallas_call x1, Pallas kernels: 114 us -> 118 us  [per_device(): pl.pallas_call(functools.partial(fused_kernel, bits, twin, block, shared_...]
    unnamed x4 -> x5, local copies, waits for them, and re-layouts: 4.19 us -> 5.54 us
where the time goes in v3:
time: 127 us
  Pallas kernels  118 us (93%)
  local copies, waits for them, and re-layouts  8.58 us (7%)
    pallas_call x1, Pallas kernels, per_device(): pl.pallas_call(functools.partial(fused_kernel, bits, twin, block, shared_...  118 us
    unnamed x5, local copies, waits for them, and re-layouts  5.54 us

profile of v3, /device:TPU:0, one launch (start us, length us, event | category | flops | bytes accessed | tf_op | source)
XLA Modules:
  0.0 127.0 jit_solution(13870304076243686165)
XLA Ops:
  0.6 1.3 %copy.9.coords_ref = s32[8,2]{1,0:T(8,128)} copy(s32[8,2]{0,1:T(2,128)} %param.9) | data formatting | bytes 128 | tf_op args[4]
  2.0 1.5 %copy.14 = bf16[2,4,8,512]{3,2,0,1:T(8,128)(2,1)} copy(bf16[2,4,8,512]{3,2,1,0:T(8,128)(2,1)} %bitcast.15) | data formatting | bytes 131072 | tf_op jit(solution)/shard_map/reshape | solution.py:304
  3.4 117.8 %fused_layer.1 = (bf16[256,4096]{1,0:T(8,128)(2,1)}, f32[64,4096]{1,0:T(8,128)}, f32[64,512]{1,0:T(8,128)}) custom-call(s32[8,2]{1,0:T(8,128)} %copy.9.coords_ref, bf16[256,4096]{1,0:T(8,128)(2,1)} %feat_hbm.1, bf16[256,4096]{1,0:T(8,128)(2,1)} %cot_hbm.1, bf16[64,4096]{1,0:T(8,128)(2,1)} %member_ref.1, bf16[64,512]{1,0:T(8,128)(2,1)} %bitcast.12), custom_call_target="tpu_custom_call" | custom-call | tf_op jit(solution)/shard_map/fused_layer/pallas_call | solution.py:307
  121.3 1.6 %copy.12 = f32[4,2,8,512]{3,2,0,1:T(8,128)} copy(f32[4,2,8,512]{3,2,1,0:T(8,128)} %bitcast.14) | data formatting | bytes 262144 | tf_op jit(solution)/shard_map/reshape | solution.py:339
  122.8 0.0 copy-start
  122.8 3.2 %copy.17 = bf16[256,4096]{1,0:T(8,128)(2,1)} copy(bf16[256,4096]{1,0:T(8,128)(2,1)} %get-tuple-element.12) | data formatting | bytes 4194304
  126.1 0.0 copy-done
  126.1 1.0 copy.18
Async XLA Ops:
  122.8 3.2 %copy-start = (f32[64,4096]{1,0:T(8,128)S(1)}, f32[64,4096]{1,0:T(8,128)}, u32[]{:S(2)}) copy-start(f32[64,4096]{1,0:T(8,128)} %get-tuple-element.13) | copy-start | bytes 3145732

commit v4 on v3

--- a/solution.py
+++ b/solution.py
@@ -11,6 +11,8 @@
 INV_ROOT_TWO_PI = 0.3989422804014327
 MESH = pl.DeviceIdType.MESH
 CHUNK_BLOCKS = 1
+GATHER_LAG = 2
+SCATTER_LAG = 2
 VMEM_BYTES = 60 * 2**20
 
 
@@ -237,9 +239,9 @@
         def _():
             action(index)
 
-    base = ahead + shared_items
-
-    @pl.loop(0, base + items + bits)
+    base = ahead * GATHER_LAG + shared_items
+
+    @pl.loop(0, base + items + bits * SCATTER_LAG)
     def _(wave):
         for k in range(ahead):
             def gather_stage(g, k=k):
@@ -247,10 +249,12 @@
                     gather_copy(g, k - 1).wait_recv()
                 gather_copy(g, k).start()
 
-            when_in_range(wave - k, gather_stage)
+            when_in_range(wave - k * GATHER_LAG, gather_stage)
         for k in range(1, bits + 1):
-            when_in_range(wave - base - k, functools.partial(scatter_stage, k=k))
-        when_in_range(wave - ahead, lambda g: gather_copy(g, ahead - 1).wait_recv())
+            when_in_range(wave - base - k * SCATTER_LAG, functools.partial(scatter_stage, k=k))
+        when_in_range(
+            wave - ahead * GATHER_LAG, lambda g: gather_copy(g, ahead - 1).wait_recv()
+        )
 
         @pl.when(wave == base - 1)
         def _():
@@ -319,7 +323,7 @@
             pltpu.VMEM((width // block, tokens, block), bf16),
             pltpu.VMEM((member_chunks, tokens, chunk), bf16),
             pltpu.VMEM((items, count, rows, chunk), bf16),
-            pltpu.VMEM((bits + 2, count, rows, chunk), f32),
+            pltpu.VMEM((bits * SCATTER_LAG + 2, count, rows, chunk), f32),
             pltpu.VMEM((items, count, rows, chunk), bf16),
             pltpu.VMEM((items, count, rows, chunk), bf16),
             pltpu.VMEM((shared_count + 1, max(tokens, block), block), f32),

time: 127 us -> 119 us (0.937)
  Pallas kernels: 118 us -> 110 us
    pallas_call x1, Pallas kernels: 118 us -> 110 us  [per_device(): pl.pallas_call(functools.partial(fused_kernel, bits, twin, block, shared_...]
where the time goes in v4:
time: 119 us
  Pallas kernels  110 us (92%)
  local copies, waits for them, and re-layouts  8.58 us (7%)
    pallas_call x1, Pallas kernels, per_device(): pl.pallas_call(functools.partial(fused_kernel, bits, twin, block, shared_...  110 us
    unnamed x5, local copies, waits for them, and re-layouts  5.54 us

profile of v4, /device:TPU:0, one launch (start us, length us, event | category | flops | bytes accessed | tf_op | source)
XLA Modules:
  0.0 118.8 jit_solution(5062921420880917147)
XLA Ops:
  0.6 1.3 %copy.9.coords_ref = s32[8,2]{1,0:T(8,128)} copy(s32[8,2]{0,1:T(2,128)} %param.9) | data formatting | bytes 128 | tf_op args[4]
  2.0 1.5 %copy.14 = bf16[2,4,8,512]{3,2,0,1:T(8,128)(2,1)} copy(bf16[2,4,8,512]{3,2,1,0:T(8,128)(2,1)} %bitcast.15) | data formatting | bytes 131072 | tf_op jit(solution)/shard_map/reshape | solution.py:308
  3.4 109.6 %fused_layer.1 = (bf16[256,4096]{1,0:T(8,128)(2,1)}, f32[64,4096]{1,0:T(8,128)}, f32[64,512]{1,0:T(8,128)}) custom-call(s32[8,2]{1,0:T(8,128)} %copy.9.coords_ref, bf16[256,4096]{1,0:T(8,128)(2,1)} %feat_hbm.1, bf16[256,4096]{1,0:T(8,128)(2,1)} %cot_hbm.1, bf16[64,4096]{1,0:T(8,128)(2,1)} %member_ref.1, bf16[64,512]{1,0:T(8,128)(2,1)} %bitcast.12), custom_call_target="tpu_custom_call" | custom-call | tf_op jit(solution)/shard_map/fused_layer/pallas_call | solution.py:311
  113.1 1.6 %copy.12 = f32[4,2,8,512]{3,2,0,1:T(8,128)} copy(f32[4,2,8,512]{3,2,1,0:T(8,128)} %bitcast.14) | data formatting | bytes 262144 | tf_op jit(solution)/shard_map/reshape | solution.py:343
  114.6 0.0 copy-start
  114.6 3.2 %copy.17 = bf16[256,4096]{1,0:T(8,128)(2,1)} copy(bf16[256,4096]{1,0:T(8,128)(2,1)} %get-tuple-element.12) | data formatting | bytes 4194304
  117.9 0.0 copy-done
  117.9 1.0 copy.18
Async XLA Ops:
  114.6 3.2 %copy-start = (f32[64,4096]{1,0:T(8,128)S(1)}, f32[64,4096]{1,0:T(8,128)}, u32[]{:S(2)}) copy-start(f32[64,4096]{1,0:T(8,128)} %get-tuple-element.13) | copy-start | bytes 3145732
